TPU v7x, 32 devices: a whole 2x2x4 slice. The times are simulated.
32 devices in a mesh: row: 4 (over z), col: 8 (over y, x, core).
Axes of the slice: x: 2, y: 2, z: 4, core: 2. Of those that a mesh axis runs over, the one named last changes fastest.
Arguments:
- points: bfloat16 [2, 8192], P(None, ('row', 'col')), may hold values from 0 to 1
- noise_var: float32 [8192], P(('row', 'col')), may hold values from 0.5 to 2
- district: int32 [8192], P(('row', 'col')), may hold values from 0 to 63, never falling along the last dimension, each value on 1 to 512 neighbouring positions
- solution: float32 [32, 8192], P(None, ('row', 'col')), may hold values from -6 to 6
- residual: float32 [32, 8192], P(None, ('row', 'col')), may hold values from -44 to 44
- direction: float32 [32, 8192], P(None, ('row', 'col')), may hold values from -44 to 44
Outputs:
- new_solution: float32 [32, 8192], P(None, ('row', 'col'))
- new_residual: float32 [32, 8192], P(None, ('row', 'col'))
- new_direction: float32 [32, 8192], P(None, ('row', 'col'))
Inputs may be any that keep to these rules, and one draw needn't show every extreme that they name: Samples are ordered by district; every district holds 1 to 512 samples and one holds exactly 512.
All inputs are finite; a program needn't handle non-finite values.
Results may differ from a plain program's by a relative error of at most 0.004.
Values may be sent and summed in bfloat16 or wider, within the bound.
No kernel may reach another device: no remote copies, remote signals or barrier semaphores. Data moves between devices by JAX's collectives and lax.ppermute only.
A program may use at most 64 MiB of HBM per device.

v0:
```python
import math
import jax
import jax.numpy as jnp
from jax import lax
from jax.sharding import PartitionSpec as P

NDIST = 64
root_three = math.sqrt(3.0)
corr_range = 0.05
district_gain = 0.5


def matern_tile(left_points, right_points):
    left_vals = left_points.astype(jnp.float32)
    right_vals = right_points.astype(jnp.float32)
    delta_x = left_vals[0][:, None] - right_vals[0][None, :]
    delta_y = left_vals[1][:, None] - right_vals[1][None, :]
    scaled = root_three / corr_range * jnp.sqrt(delta_x * delta_x + delta_y * delta_y)
    return ((1.0 + scaled) * jnp.exp(-scaled)).astype(jnp.bfloat16)


def small_product(left, right):
    return jnp.dot(left, right, precision=lax.Precision.HIGHEST, preferred_element_type=jnp.float32)


def chol_solve(matrix, rhs_mat):
    factor = jnp.linalg.cholesky(matrix)
    return jax.scipy.linalg.cho_solve((factor, True), rhs_mat)


def per_device(points, noise_var, district, solution, residual, direction):
    local_count = points.shape[1]
    rhs_count = direction.shape[0]
    whole_count = local_count * lax.axis_size("row") * lax.axis_size("col")
    kernel_scale = 1.0 / (corr_range * math.sqrt(whole_count))
    labels = jnp.arange(NDIST, dtype=jnp.int32)
    onehot = (district[None, :] == labels[:, None]).astype(jnp.float32)
    local_sums = small_product(direction, onehot.T)
    local_sizes = jnp.sum(onehot, axis=1)
    local_norm = small_product(residual, residual.T)
    district_sums, sizes = lax.psum((local_sums, local_sizes), ("row", "col"))
    old_norm = lax.psum(local_norm, ("row", "col"))
    lowered = direction.astype(jnp.bfloat16)
    empty = jnp.zeros((rhs_count, local_count), jnp.float32)
    left_points = lax.all_gather(points, ("row", "col"), axis=1, tiled=True)
    left_dir = lax.all_gather(lowered, ("row", "col"), axis=1, tiled=True)
    width_now = left_points.shape[1]
    block_len = 8192

    def one_step(index_now, acc):
        part_points = lax.dynamic_slice_in_dim(left_points, index_now * block_len, block_len, 1)
        part_dir = lax.dynamic_slice_in_dim(left_dir, index_now * block_len, block_len, 1)
        return acc + jnp.dot(
            part_dir, matern_tile(part_points, points), preferred_element_type=jnp.float32
        )

    kernel_part = lax.fori_loop(0, width_now // block_len, one_step, empty)
    weights = district_sums / jnp.sqrt(sizes)[None, :]
    district_part = small_product(weights, onehot)
    image = (
        noise_var[None, :] * direction + kernel_part * kernel_scale + district_gain * district_part
    )
    local_curv = small_product(direction, image.T)
    curvature = lax.psum(local_curv, ("row", "col"))
    alpha = chol_solve(curvature, old_norm)
    new_solution = solution + small_product(alpha.T, direction)
    new_residual = residual - small_product(alpha.T, image)
    new_norm = lax.psum(small_product(new_residual, new_residual.T), ("row", "col"))
    beta = chol_solve(old_norm, new_norm)
    new_direction = new_residual + small_product(beta.T, direction)
    return (new_solution, new_residual, new_direction)


def solution(mesh):
    in_specs = (
        P(None, ("row", "col")),
        P(("row", "col")),
        P(("row", "col")),
        P(None, ("row", "col")),
        P(None, ("row", "col")),
        P(None, ("row", "col")),
    )
    out_specs = (P(None, ("row", "col")), P(None, ("row", "col")), P(None, ("row", "col")))
    return jax.shard_map(
        per_device, mesh=mesh, in_specs=in_specs, out_specs=out_specs, check_vma=False
    )
```

profile of v0, /device:TPU:14, one launch (start us, length us, event | category | flops | bytes accessed | tf_op | source)
XLA Modules:
  0.0 224.8 jit_solution(12056123770513564116)
XLA Ops:
  0.6 0.0 copy-start
  0.6 0.0 copy-start.5
  0.7 29.1 %all_gather.6 = bf16[2,8192]{1,0:T(2,128)(2,1)S(1)} all-gather(bf16[2,256]{1,0:T(2,128)(2,1)} %param.9), channel_id=1, replica_groups=mesh['row'=4,'col'=8] {'row','col'}, dimensions={1}, use_global_device_ids=true | all-gather | bytes 33792 | tf_op jit(solution)/shard_map/all_gather | solution.py:45
  29.8 0.8 fusion.24
  30.5 0.8 convert_element_type.21
  31.3 41.2 %all_gather.7 = bf16[32,8192]{1,0:T(8,128)(2,1)S(1)} all-gather(bf16[32,256]{1,0:T(8,128)(2,1)S(1)} %convert_element_type.21), channel_id=1, replica_groups=mesh['row'=4,'col'=8] {'row','col'}, dimensions={1}, use_global_device_ids=true | all-gather | bytes 540672 | tf_op jit(solution)/shard_map/all_gather | solution.py:46
  72.5 0.0 copy-done
  72.5 0.0 copy-done.5
  72.5 0.0 copy-start.4
  72.5 0.0 copy-start.2
  72.5 5.2 %fusion.4 = f32[32,256]{1,0:T(8,128)S(1)} fusion(bf16[32,8192]{1,0:T(8,128)(2,1)S(1)} %all_gather.7, f32[256]{0:T(256)S(1)} %bitcast.55, f32[8192]{0:T(1024)S(1)} %bitcast.53, f32[256]{0:T(256)S(1)} %bitcast.54, f32[8192]{0:T(1024)S(1)} %bitcast.52, f32[32,256]{1,0:T(8,128)S(1)} %copy-done, f32[256]{0:T(256)S(1)} %copy-done.5), kind=kOutput, calls=%fused_computation.10 | convolution fusion | flops 155213824 | bytes 658432 | tf_op jit(solution)/shard_map/while/body/eval_jaxpr/dot_general | solution.py:53
  77.7 0.0 copy-done.4
  77.7 0.2 convolution_bitcast_fusion
  77.9 0.1 convert_reduce_fusion
  78.0 49.4 %all-reduce.1 = (f32[32,64]{0,1:T(8,128)S(1)}, f32[64]{0:T(128)S(1)}) all-reduce(f32[32,64]{0,1:T(8,128)S(1)} %convolution_bitcast_fusion, f32[64]{0:T(128)S(1)} %convert_reduce_fusion), channel_id=1, replica_groups=mesh['row'=4,'col'=8] {'row','col'}, use_global_device_ids=true, to_apply=%region_0.0 | all-reduce | flops 2112 | bytes 16896 | tf_op jit(solution)/shard_map/psum | solution.py:41
  127.3 0.3 fusion.1
  127.6 0.0 copy-start.3
  127.6 0.2 convolution_bitcast_fusion.1
  127.8 0.0 copy-done.2
  127.8 0.2 fusion.25
  128.0 38.5 %all-reduce = (f32[32,32]{0,1:T(8,128)S(1)}, f32[32,32]{0,1:T(8,128)S(1)}) all-reduce(f32[32,32]{0,1:T(8,128)S(1)} %fusion.25, f32[32,32]{0,1:T(8,128)S(1)} %convolution_bitcast_fusion.1), channel_id=1, replica_groups=mesh['row'=4,'col'=8] {'row','col'}, use_global_device_ids=true, to_apply=%region_6.8 | all-reduce | flops 2048 | bytes 16384 | tf_op jit(solution)/shard_map/psum | solution.py:42
  166.5 0.1 copy.14
  166.6 0.1 copy.12
  166.6 2.9 %cholesky.55 = f32[32,32]{1,0:T(8,128)S(1)} custom-call(f32[32,32]{1,0:T(8,128)S(1)} %get-tuple-element.31), custom_call_target="Cholesky" | custom-call | tf_op jit(solution)/shard_map/jit(cholesky)/cholesky | solution.py:27
  169.6 0.6 compare_reduce_fusion
  170.2 0.7 fusion.9
  170.9 2.4 %custom-call.9 = f32[1,32,32]{1,2,0:T(8,128)S(1)} custom-call(f32[1,32,32]{2,1,0:T(8,128)S(1)} %fusion.9), custom_call_target="InvertDiagBlocksLowerTriangular" | custom-call | tf_op jit(solution)/shard_map/jit(_cho_solve)/triangular_solve | solution.py:28
  173.3 2.9 %cholesky.44 = f32[32,32]{1,0:T(8,128)S(1)} custom-call(f32[32,32]{1,0:T(8,128)S(1)} %get-tuple-element.32), custom_call_target="Cholesky" | custom-call | tf_op jit(solution)/shard_map/jit(cholesky)/cholesky | solution.py:27
  176.3 0.6 compare_reduce_fusion.1
  176.9 0.7 fusion.8
  177.6 2.4 %custom-call.8 = f32[1,32,32]{1,2,0:T(8,128)S(1)} custom-call(f32[1,32,32]{2,1,0:T(8,128)S(1)} %fusion.8), custom_call_target="InvertDiagBlocksLowerTriangular" | custom-call | tf_op jit(solution)/shard_map/jit(_cho_solve)/triangular_solve | solution.py:28
  180.0 0.2 fusion.17
  180.3 0.1 fusion.15
  180.4 0.2 convolution_subtract_fusion
  180.7 0.0 copy-start.1
  180.7 0.2 fusion.26
  180.8 41.9 %psum.39 = f32[32,32]{1,0:T(8,128)S(1)} all-reduce(f32[32,32]{1,0:T(8,128)S(1)} %fusion.26), channel_id=1, replica_groups=mesh['row'=4,'col'=8] {'row','col'}, use_global_device_ids=true, to_apply=%region_7.0 | all-reduce | flops 1024 | bytes 8192 | tf_op jit(solution)/shard_map/psum | solution.py:68
  222.7 0.2 fusion.12
  222.9 0.1 fusion.10
  223.1 0.9 convolution_add_fusion
  223.9 0.0 copy-done.3
  223.9 0.8 convolution_add_fusion.1
  224.8 0.0 copy-done.1
  (5 shorter events, 0.1 us)
Async XLA Ops:
  0.6 71.8 %copy-start = (f32[32,256]{1,0:T(8,128)S(1)}, f32[32,256]{1,0:T(8,128)}, u32[]{:S(2)}) copy-start(f32[32,256]{1,0:T(8,128)} %param.14) | copy-start | bytes 98308
  0.6 71.8 %copy-start.5 = (f32[256]{0:T(256)S(1)}, f32[256]{0:T(256)}, u32[]{:S(2)}) copy-start(f32[256]{0:T(256)} %param.10) | copy-start | bytes 3076
  72.5 5.2 %copy-start.4 = (s32[256]{0:T(256)S(1)}, s32[256]{0:T(256)}, u32[]{:S(2)}) copy-start(s32[256]{0:T(256)} %param.11) | copy-start | bytes 3076
  72.5 55.3 %copy-start.2 = (f32[32,256]{1,0:T(8,128)S(1)}, f32[32,256]{1,0:T(8,128)}, u32[]{:S(2)}) copy-start(f32[32,256]{1,0:T(8,128)} %param.13) | copy-start | bytes 98308
  127.6 96.3 %copy-start.3 = (f32[32,256]{1,0:T(8,128)S(1)}, f32[32,256]{1,0:T(8,128)}, u32[]{:S(2)}) copy-start(f32[32,256]{1,0:T(8,128)} %param.12) | copy-start | bytes 98308
  180.7 44.1 %copy-start.1 = (f32[32,256]{1,0:T(8,128)}, f32[32,256]{1,0:T(8,128)S(1)}, u32[]{:S(2)}) copy-start(f32[32,256]{1,0:T(8,128)S(1)} %convolution_subtract_fusion) | copy-start | bytes 98308
where the time goes:
time: 225 us
  blocking collectives  200 us (89%)
  other arithmetic  14.3 us (6%)
  matrix products  8.78 us (4%)
    psum x1, blocking collectives, per_device(): district_sums, sizes = lax.psum((local_sums, local_sizes), ('row', 'col'))  49.4 us
    psum x1, blocking collectives, per_device(): lax.psum(small_product(new_residual, new_residual.T), ('row', 'col'))  41.9 us
    all_gather x1, blocking collectives, per_device(): left_dir = lax.all_gather(lowered, ('row', 'col'), axis=1, tiled=True)  41.2 us
    psum x1, blocking collectives, per_device(): old_norm = lax.psum(local_norm, ('row', 'col'))  38.5 us
    all_gather x1, blocking collectives, per_device(): left_points = lax.all_gather(points, ('row', 'col'), axis=1, tiled=True)  29.1 us
    another operation x6, other arithmetic, chol_solve(): factor = jnp.linalg.cholesky(matrix)  7.2 us
    another operation x4, other arithmetic, chol_solve(): return jax.scipy.linalg.cho_solve((factor, True), rhs_mat)  6.17 us
    dot_general x1, matrix products, one_step(): jnp.dot(part_dir, matern_tile(part_points, points), preferred_element_typ...  5.2 us

commit v1 on v0

--- a/solution.py
+++ b/solution.py
@@ -1,3 +1,4 @@
+import functools
 import math
 import jax
 import jax.numpy as jnp
@@ -8,6 +9,32 @@
 root_three = math.sqrt(3.0)
 corr_range = 0.05
 district_gain = 0.5
+
+
+def push_the_slabs(x_in, d0):
+    later, big, answer = (
+        lax.psum(1, ("row", "col")),
+        lax.axis_index(("row", "col")),
+        x_in.shape[d0],
+    )
+    last, y_new = (x_in, 1)
+    while y_new < later:
+        last = jnp.concatenate(
+            [
+                last,
+                lax.ppermute(
+                    last,
+                    ("row", "col"),
+                    list(map(lambda j0: (j0, (j0 - y_new) % later), range(later))),
+                ),
+            ],
+            d0,
+        )
+        y_new = 2 * y_new
+    return jnp.roll(last, big * answer, d0)
+
+
+build_chunk = functools.partial(push_the_slabs, d0=1)
 
 
 def matern_tile(left_points, right_points):
@@ -42,7 +69,7 @@
     old_norm = lax.psum(local_norm, ("row", "col"))
     lowered = direction.astype(jnp.bfloat16)
     empty = jnp.zeros((rhs_count, local_count), jnp.float32)
-    left_points = lax.all_gather(points, ("row", "col"), axis=1, tiled=True)
+    left_points = build_chunk(points)
     left_dir = lax.all_gather(lowered, ("row", "col"), axis=1, tiled=True)
     width_now = left_points.shape[1]
     block_len = 8192

time: 225 us -> 209 us (0.929); the launches traced: 225 us -> 205 us
  blocking collectives: 200 us -> 152 us
  starting transfers between devices: 0 us -> 20.3 us
  waiting for transfers between devices: 0 us -> 7.48 us
    all_gather x1 -> x0, blocking collectives: 29.1 us -> none  [per_device(): left_points = lax.all_gather(points, ('row', 'col'), axis=1, tiled=True)]
    ppermute x0 -> x5, starting transfers between devices: none -> 20.3 us  [push_the_slabs(): lax.ppermute(last, ('row', 'col'), list(map(lambda j0: (j0, (j0 - y_new)...]
    psum x1, blocking collectives: 49.4 us -> 38.3 us  [per_device(): district_sums, sizes = lax.psum((local_sums, local_sizes), ('row', 'col'))]
    all_gather x1, blocking collectives: 41.2 us -> 33.2 us  [per_device(): left_dir = lax.all_gather(lowered, ('row', 'col'), axis=1, tiled=True)]
    ppermute x0 -> x5, waiting for transfers between devices: none -> 7.48 us  [push_the_slabs(): lax.ppermute(last, ('row', 'col'), list(map(lambda j0: (j0, (j0 - y_new)...]
    psum x1, blocking collectives: 38.5 us -> 42.3 us  [per_device(): old_norm = lax.psum(local_norm, ('row', 'col'))]
    psum x1, blocking collectives: 41.9 us -> 38.2 us  [per_device(): lax.psum(small_product(new_residual, new_residual.T), ('row', 'col'))]
  transfers between devices with their start and end apart: 0 -> 5, of which waited for: 0 -> 3; matrix products, arithmetic and copies ran while one was open for 0% -> 1% of each run, Pallas kernels for 0% -> 0%
where the time goes in v1:
time: 209 us; the launch traced here: 205 us
  blocking collectives  152 us (73%)
  starting transfers between devices  20.3 us (10%)
  other arithmetic  14.3 us (7%)
  matrix products  8.77 us (4%)
  waiting for transfers between devices  7.48 us (4%)
    psum x1, blocking collectives, per_device(): old_norm = lax.psum(local_norm, ('row', 'col'))  42.3 us
    psum x1, blocking collectives, per_device(): district_sums, sizes = lax.psum((local_sums, local_sizes), ('row', 'col'))  38.3 us
    psum x1, blocking collectives, per_device(): lax.psum(small_product(new_residual, new_residual.T), ('row', 'col'))  38.2 us
    all_gather x1, blocking collectives, per_device(): left_dir = lax.all_gather(lowered, ('row', 'col'), axis=1, tiled=True)  33.2 us
    ppermute x5, starting transfers between devices, push_the_slabs(): lax.ppermute(last, ('row', 'col'), list(map(lambda j0: (j0, (j0 - y_new)...  20.3 us
    ppermute x5, waiting for transfers between devices, push_the_slabs(): lax.ppermute(last, ('row', 'col'), list(map(lambda j0: (j0, (j0 - y_new)...  7.48 us
    another operation x6, other arithmetic, chol_solve(): factor = jnp.linalg.cholesky(matrix)  7.2 us
    another operation x4, other arithmetic, chol_solve(): return jax.scipy.linalg.cho_solve((factor, True), rhs_mat)  6.17 us
  transfers between devices with their start and end apart: 5, of which 3 were waited for; matrix products, arithmetic and copies ran while one was open for 1% of the time, Pallas kernels for 0%

profile of v1, /device:TPU:14, one launch (start us, length us, event | category | flops | bytes accessed | tf_op | source)
XLA Modules:
  0.0 205.0 jit_solution(15118393742832450573)
XLA Ops:
  0.6 0.0 copy-start.3
  0.6 0.0 copy-start
  0.7 0.0 copy-start.5
  0.7 0.0 copy-start.2
  0.7 0.1 collective-permute-start
  0.7 0.7 fusion.24
  1.5 0.8 convert_element_type.21
  2.2 0.0 copy-start.6
  2.2 33.2 %all_gather.3 = bf16[32,8192]{1,0:T(8,128)(2,1)S(1)} all-gather(bf16[32,256]{1,0:T(8,128)(2,1)S(1)} %convert_element_type.21), channel_id=1, replica_groups=mesh['row'=4,'col'=8] {'row','col'}, dimensions={1}, use_global_device_ids=true | all-gather | bytes 540672 | tf_op jit(solution)/shard_map/all_gather | solution.py:73
  35.5 0.0 copy-done
  35.5 0.0 copy-done.5
  35.5 0.2 convolution_bitcast_fusion
  35.6 0.0 copy-done.2
  35.7 0.2 fusion.25
  35.8 0.0 copy-done.3
  35.8 0.0 collective-permute-done
  35.9 0.6 collective-permute-start.1
  36.5 4.8 %collective-permute-done.1 = bf16[2,512]{1,0:T(2,128)(2,1)S(1)} collective-permute-done((bf16[2,512]{1,0:T(2,128)(2,1)S(1)}, bf16[2,512]{1,0:T(2,128)(2,1)S(1)}, u32[]{:S(2)}, u32[]{:S(2)}) %collective-permute-start.1) | collective-permute-done | bytes 2080 | tf_op jit(solution)/shard_map/ppermute | solution.py:25
  41.3 3.3 %collective-permute-start.2 = (bf16[2,1024]{1,0:T(2,128)(2,1)S(1)}, bf16[2,1024]{1,0:T(2,128)(2,1)S(1)}, u32[]{:S(2)}, u32[]{:S(2)}) collective-permute-start(bf16[2,1024]{1,0:T(2,128)(2,1)S(1)} %pad_maximum_fusion.1), channel_id=1, source_target_pairs={{0,28},{1,29},{2,30},{3,31},{4,0},{5,1},{6,2},{7,3},{8,4},{9,5},{1... | collective-permute-start | bytes 12296 | tf_op jit(solution)/shard_map/ppermute | solution.py:25
  44.6 1.3 collective-permute-done.2
  46.0 6.9 %collective-permute-start.3 = (bf16[2,2048]{1,0:T(2,128)(2,1)S(1)}, bf16[2,2048]{1,0:T(2,128)(2,1)S(1)}, u32[]{:S(2)}, u32[]{:S(2)}) collective-permute-start(bf16[2,2048]{1,0:T(2,128)(2,1)S(1)} %pad_maximum_fusion), channel_id=1, source_target_pairs={{0,24},{1,25},{2,26},{3,27},{4,28},{5,29},{6,30},{7,31},{8,0},{9,1... | collective-permute-start | bytes 24584 | tf_op jit(solution)/shard_map/ppermute | solution.py:25
  52.9 1.4 collective-permute-done.3
  54.3 9.5 %collective-permute-start.4 = (bf16[2,4096]{1,0:T(2,128)(2,1)S(1)}, bf16[2,4096]{1,0:T(2,128)(2,1)S(1)}, u32[]{:S(2)}, u32[]{:S(2)}) collective-permute-start(bf16[2,4096]{1,0:T(2,128)(2,1)S(1)} %get-tuple-element.29), channel_id=1, source_target_pairs={{0,16},{1,17},{2,18},{3,19},{4,20},{5,21},{6,22},{7,23},{8,24},{9,... | collective-permute-start | bytes 49160 | tf_op jit(solution)/shard_map/ppermute | solution.py:25
  63.7 0.1 convert_reduce_fusion
  63.8 38.3 %all-reduce.1 = (f32[32,64]{0,1:T(8,128)S(1)}, f32[64]{0:T(128)S(1)}) all-reduce(f32[32,64]{0,1:T(8,128)S(1)} %convolution_bitcast_fusion, f32[64]{0:T(128)S(1)} %convert_reduce_fusion), channel_id=1, replica_groups=mesh['row'=4,'col'=8] {'row','col'}, use_global_device_ids=true, to_apply=%region_0.0 | all-reduce | flops 2112 | bytes 16896 | tf_op jit(solution)/shard_map/psum | solution.py:68
  102.2 0.0 collective-permute-done.4
  102.4 0.1 fusion.23
  102.4 0.0 copy-done.6
  102.4 5.2 %fusion.4 = f32[32,256]{1,0:T(8,128)S(1)} fusion(bf16[32,8192]{1,0:T(8,128)(2,1)S(1)} %all_gather.3, f32[256]{0:T(256)S(1)} %bitcast.55, f32[8192]{0:T(1024)S(1)} %bitcast.53, f32[256]{0:T(256)S(1)} %bitcast.54, f32[8192]{0:T(1024)S(1)} %bitcast.52, f32[32,256]{1,0:T(8,128)S(1)} %copy-done, f32[256]{0:T(256)S(1)} %copy-done.6), kind=kOutput, calls=%fused_computation.10 | convolution fusion | flops 155213824 | bytes 658432 | tf_op jit(solution)/shard_map/while/body/eval_jaxpr/dot_general | solution.py:80
  107.6 0.0 copy-start.4
  107.6 0.3 fusion.1
  107.9 0.2 convolution_bitcast_fusion.1
  108.1 42.3 %all-reduce = (f32[32,32]{0,1:T(8,128)S(1)}, f32[32,32]{0,1:T(8,128)S(1)}) all-reduce(f32[32,32]{0,1:T(8,128)S(1)} %fusion.25, f32[32,32]{0,1:T(8,128)S(1)} %convolution_bitcast_fusion.1), channel_id=1, replica_groups=mesh['row'=4,'col'=8] {'row','col'}, use_global_device_ids=true, to_apply=%region_6.8 | all-reduce | flops 2048 | bytes 16384 | tf_op jit(solution)/shard_map/psum | solution.py:69
  150.4 0.1 copy.12
  150.4 0.1 copy.14
  150.5 2.9 %cholesky.55 = f32[32,32]{1,0:T(8,128)S(1)} custom-call(f32[32,32]{1,0:T(8,128)S(1)} %get-tuple-element.41), custom_call_target="Cholesky" | custom-call | tf_op jit(solution)/shard_map/jit(cholesky)/cholesky | solution.py:54
  153.5 0.6 compare_reduce_fusion
  154.1 0.7 fusion.9
  154.8 2.4 %custom-call.9 = f32[1,32,32]{1,2,0:T(8,128)S(1)} custom-call(f32[1,32,32]{2,1,0:T(8,128)S(1)} %fusion.9), custom_call_target="InvertDiagBlocksLowerTriangular" | custom-call | tf_op jit(solution)/shard_map/jit(_cho_solve)/triangular_solve | solution.py:55
  157.2 2.9 %cholesky.44 = f32[32,32]{1,0:T(8,128)S(1)} custom-call(f32[32,32]{1,0:T(8,128)S(1)} %get-tuple-element.42), custom_call_target="Cholesky" | custom-call | tf_op jit(solution)/shard_map/jit(cholesky)/cholesky | solution.py:54
  160.2 0.6 compare_reduce_fusion.1
  160.8 0.7 fusion.8
  161.5 2.4 %custom-call.8 = f32[1,32,32]{1,2,0:T(8,128)S(1)} custom-call(f32[1,32,32]{2,1,0:T(8,128)S(1)} %fusion.8), custom_call_target="InvertDiagBlocksLowerTriangular" | custom-call | tf_op jit(solution)/shard_map/jit(_cho_solve)/triangular_solve | solution.py:55
  163.9 0.2 fusion.17
  164.2 0.1 fusion.15
  164.3 0.2 convolution_subtract_fusion
  164.6 0.0 copy-start.1
  164.6 0.2 fusion.26
  164.7 38.2 %psum.39 = f32[32,32]{1,0:T(8,128)S(1)} all-reduce(f32[32,32]{1,0:T(8,128)S(1)} %fusion.26), channel_id=1, replica_groups=mesh['row'=4,'col'=8] {'row','col'}, use_global_device_ids=true, to_apply=%region_7.10 | all-reduce | flops 1024 | bytes 8192 | tf_op jit(solution)/shard_map/psum | solution.py:95
  203.0 0.2 fusion.12
  203.2 0.1 fusion.10
  203.3 0.9 convolution_add_fusion
  204.2 0.0 copy-done.4
  204.2 0.8 convolution_add_fusion.1
  205.0 0.0 copy-done.1
  (20 shorter events, 0.3 us)
Async XLA Ops:
  0.6 35.2 %copy-start.3 = (bf16[2,256]{1,0:T(2,128)(2,1)S(1)}, bf16[2,256]{1,0:T(2,128)(2,1)}, u32[]{:S(2)}) copy-start(bf16[2,256]{1,0:T(2,128)(2,1)} %param.9) | copy-start | bytes 3076
  0.6 34.8 %copy-start = (f32[32,256]{1,0:T(8,128)S(1)}, f32[32,256]{1,0:T(8,128)}, u32[]{:S(2)}) copy-start(f32[32,256]{1,0:T(8,128)} %param.14) | copy-start | bytes 98308
  0.7 34.8 %copy-start.5 = (s32[256]{0:T(256)S(1)}, s32[256]{0:T(256)}, u32[]{:S(2)}) copy-start(s32[256]{0:T(256)} %param.11) | copy-start | bytes 3076
  0.7 35.0 %copy-start.2 = (f32[32,256]{1,0:T(8,128)S(1)}, f32[32,256]{1,0:T(8,128)}, u32[]{:S(2)}) copy-start(f32[32,256]{1,0:T(8,128)} %param.13) | copy-start | bytes 98308
  0.7 35.2 %collective-permute-start = (bf16[2,256]{1,0:T(2,128)(2,1)}, bf16[2,256]{1,0:T(2,128)(2,1)S(1)}, u32[]{:S(2)}, u32[]{:S(2)}) collective-permute-start(bf16[2,256]{1,0:T(2,128)(2,1)} %param.9), channel_id=1, source_target_pairs={{0,31},{1,0},{2,1},{3,2},{4,3},{5,4},{6,5},{7,6},{8,7},{9,8},{10,9... | collective-permute-start | bytes 3080 | tf_op jit(solution)/shard_map/ppermute | solution.py:25
  2.2 100.2 %copy-start.6 = (f32[256]{0:T(256)S(1)}, f32[256]{0:T(256)}, u32[]{:S(2)}) copy-start(f32[256]{0:T(256)} %param.10) | copy-start | bytes 3076
  35.9 5.4 %collective-permute-start.1 = (bf16[2,512]{1,0:T(2,128)(2,1)S(1)}, bf16[2,512]{1,0:T(2,128)(2,1)S(1)}, u32[]{:S(2)}, u32[]{:S(2)}) collective-permute-start(bf16[2,512]{1,0:T(2,128)(2,1)S(1)} %pad_maximum_fusion.2), channel_id=1, source_target_pairs={{0,30},{1,31},{2,0},{3,1},{4,2},{5,3},{6,4},{7,5},{8,6},{9,7},{10,... | collective-permute-start | bytes 6152 | tf_op jit(solution)/shard_map/ppermute | solution.py:25
  41.3 4.6 %collective-permute-start.2 = (bf16[2,1024]{1,0:T(2,128)(2,1)S(1)}, bf16[2,1024]{1,0:T(2,128)(2,1)S(1)}, u32[]{:S(2)}, u32[]{:S(2)}) collective-permute-start(bf16[2,1024]{1,0:T(2,128)(2,1)S(1)} %pad_maximum_fusion.1), channel_id=1, source_target_pairs={{0,28},{1,29},{2,30},{3,31},{4,0},{5,1},{6,2},{7,3},{8,4},{9,5},{1... | collective-permute-start | bytes 12296 | tf_op jit(solution)/shard_map/ppermute | solution.py:25
  46.0 8.3 %collective-permute-start.3 = (bf16[2,2048]{1,0:T(2,128)(2,1)S(1)}, bf16[2,2048]{1,0:T(2,128)(2,1)S(1)}, u32[]{:S(2)}, u32[]{:S(2)}) collective-permute-start(bf16[2,2048]{1,0:T(2,128)(2,1)S(1)} %pad_maximum_fusion), channel_id=1, source_target_pairs={{0,24},{1,25},{2,26},{3,27},{4,28},{5,29},{6,30},{7,31},{8,0},{9,1... | collective-permute-start | bytes 24584 | tf_op jit(solution)/shard_map/ppermute | solution.py:25
  54.3 47.9 %collective-permute-start.4 = (bf16[2,4096]{1,0:T(2,128)(2,1)S(1)}, bf16[2,4096]{1,0:T(2,128)(2,1)S(1)}, u32[]{:S(2)}, u32[]{:S(2)}) collective-permute-start(bf16[2,4096]{1,0:T(2,128)(2,1)S(1)} %get-tuple-element.29), channel_id=1, source_target_pairs={{0,16},{1,17},{2,18},{3,19},{4,20},{5,21},{6,22},{7,23},{8,24},{9,... | collective-permute-start | bytes 49160 | tf_op jit(solution)/shard_map/ppermute | solution.py:25
  107.6 96.5 %copy-start.4 = (f32[32,256]{1,0:T(8,128)S(1)}, f32[32,256]{1,0:T(8,128)}, u32[]{:S(2)}) copy-start(f32[32,256]{1,0:T(8,128)} %param.12) | copy-start | bytes 98308
  164.6 40.5 %copy-start.1 = (f32[32,256]{1,0:T(8,128)}, f32[32,256]{1,0:T(8,128)S(1)}, u32[]{:S(2)}) copy-start(f32[32,256]{1,0:T(8,128)S(1)} %convolution_subtract_fusion) | copy-start | bytes 98308
